TPU v7x, 32 devices: a whole 2x2x4 slice. The times are simulated.
32 devices in a mesh: expert: 16 (over z, x, core), tensor: 2 (over y).
Axes of the slice: x: 2, y: 2, z: 4, core: 2. Of those that a mesh axis runs over, the one named last changes fastest.
Arguments:
- tokens: bfloat16 [2048, 2048], P('expert', 'tensor'), may hold values from -6 to 6
- cotangent: bfloat16 [2048, 2048], P('expert', 'tensor'), may hold values from -6 to 6
- route_ids: int32 [2048, 6], P('expert'), may hold values from 0 to 15, all different within a row
- route_weights: float32 [2048, 6], P('expert'), may hold values from 0.05 to 0.5
- shared_gate: bfloat16 [1408, 2048], P('tensor'), may hold values from -0.125 to 0.125
- shared_up: bfloat16 [1408, 2048], P('tensor'), may hold values from -0.125 to 0.125
- shared_down: bfloat16 [1408, 2048], P('tensor'), may hold values from -0.15625 to 0.15625
- expert_gate: bfloat16 [16, 1408, 2048], P('expert', 'tensor'), may hold values from -0.125 to 0.125
- expert_up: bfloat16 [16, 1408, 2048], P('expert', 'tensor'), may hold values from -0.125 to 0.125
- expert_down: bfloat16 [16, 1408, 2048], P('expert', 'tensor'), may hold values from -0.15625 to 0.15625
Outputs:
- layer_output: bfloat16 [2048, 2048], P('expert', 'tensor')
- input_grad: bfloat16 [2048, 2048], P('expert', 'tensor')
Inputs may be any that keep to these rules, and one draw needn't show every extreme that they name: `route_ids`: each row names 6 different experts.
All inputs are finite; a program needn't handle non-finite values.
Results may differ from a plain program's by a relative error of at most 0.0051.
Values may be sent and summed in bfloat16 or wider, within the bound.
No kernel may reach another device: no remote copies, remote signals or barrier semaphores. Data moves between devices by JAX's collectives and lax.ppermute only.
A program may use at most 64 MiB of HBM per device.

v0:
```python
import jax
import jax.numpy as jnp
from jax import lax
from jax.sharding import PartitionSpec as P


def silu_parts(pre_act):
    sigmoid_value = jax.nn.sigmoid(pre_act)
    return (pre_act * sigmoid_value, sigmoid_value * (1.0 + pre_act * (1.0 - sigmoid_value)))


def on_device(
    tokens,
    cotangent,
    route_ids,
    route_weights,
    shared_gate,
    shared_up,
    shared_down,
    expert_gate,
    expert_up,
    expert_down,
):
    expert_count = lax.axis_size("expert")
    tok_rows, top_count = route_ids.shape
    local_experts = expert_gate.shape[0]
    all_experts = local_experts * expert_count
    capacity = tok_rows * top_count // (2 * all_experts)
    slot_total = all_experts * capacity
    flat_ids = route_ids.reshape(-1)
    one_hot = (flat_ids[:, None] == jnp.arange(all_experts, dtype=jnp.int32)[None, :]).astype(
        jnp.int32
    )
    rank_in = jnp.sum((jnp.cumsum(one_hot, axis=0) - one_hot) * one_hot, axis=1)
    kept_mask = rank_in < capacity
    slot_index = jnp.where(kept_mask, flat_ids * capacity + rank_in, slot_total)
    slot_match = jnp.arange(slot_total, dtype=jnp.int32)[:, None] == slot_index[None, :]
    dispatch = jnp.any(slot_match.reshape(slot_total, tok_rows, top_count), axis=2).astype(
        jnp.bfloat16
    )
    gate_flat = route_weights.reshape(-1)
    slot_gate = jnp.sum(jnp.where(slot_match, gate_flat[None, :], 0.0), axis=1)
    gate_dispatch = dispatch.astype(jnp.float32) * slot_gate[:, None]
    x_full, c_full = (
        lax.all_gather(tokens, "tensor", axis=1, tiled=True),
        lax.all_gather(cotangent, "tensor", axis=1, tiled=True),
    )
    x_slots = jnp.dot(dispatch, tokens, preferred_element_type=jnp.float32).astype(jnp.bfloat16)
    g_slots = (
        slot_gate[:, None] * jnp.dot(dispatch, cotangent, preferred_element_type=jnp.float32)
    ).astype(jnp.bfloat16)
    x_part, g_part = (
        lax.all_to_all(x_slots, "expert", split_axis=0, concat_axis=0, tiled=True),
        lax.all_to_all(g_slots, "expert", split_axis=0, concat_axis=0, tiled=True),
    )
    x_recv, g_recv = (
        lax.all_gather(x_part, "tensor", axis=1, tiled=True),
        lax.all_gather(g_part, "tensor", axis=1, tiled=True),
    )

    def owner_layout(values):
        shaped = values.reshape(expert_count, local_experts, capacity, values.shape[-1])
        return shaped.transpose(1, 0, 2, 3).reshape(
            local_experts, expert_count * capacity, values.shape[-1]
        )

    def source_layout(values):
        shaped = values.reshape(local_experts, expert_count, capacity, values.shape[-1])
        return shaped.transpose(1, 0, 2, 3).reshape(slot_total, values.shape[-1])

    x_own = owner_layout(x_recv)
    g_own = owner_layout(g_recv)
    gate_pre = jnp.einsum("erd,efd->erf", x_own, expert_gate, preferred_element_type=jnp.float32)
    up_pre = jnp.einsum("erd,efd->erf", x_own, expert_up, preferred_element_type=jnp.float32)
    act_value, act_slope = silu_parts(gate_pre)
    hidden = (act_value * up_pre).astype(jnp.bfloat16)
    grad_hidden = jnp.einsum("erd,efd->erf", g_own, expert_down, preferred_element_type=jnp.float32)
    grad_gate = (grad_hidden * up_pre * act_slope).astype(jnp.bfloat16)
    grad_up = (grad_hidden * act_value).astype(jnp.bfloat16)
    value_part = source_layout(
        jnp.einsum("erf,efd->erd", hidden, expert_down, preferred_element_type=jnp.float32).astype(
            jnp.bfloat16
        )
    )
    grads_joined = jnp.concatenate((grad_gate, grad_up), axis=2)
    weights_joined = jnp.concatenate((expert_gate, expert_up), axis=1)
    input_term = jnp.einsum(
        "erf,efd->erd", grads_joined, weights_joined, preferred_element_type=jnp.float32
    )
    input_part = source_layout(input_term.astype(jnp.bfloat16))
    shared_gate_pre = jnp.einsum(
        "td,fd->tf", x_full, shared_gate, preferred_element_type=jnp.float32
    )
    shared_up_pre = jnp.einsum("td,fd->tf", x_full, shared_up, preferred_element_type=jnp.float32)
    shared_act, shared_slope = silu_parts(shared_gate_pre)
    shared_hidden = (shared_act * shared_up_pre).astype(jnp.bfloat16)
    shared_value = jnp.dot(shared_hidden, shared_down, preferred_element_type=jnp.float32)
    shared_grad_hidden = jnp.einsum(
        "td,fd->tf", c_full, shared_down, preferred_element_type=jnp.float32
    )
    shared_grad_gate = (shared_grad_hidden * shared_up_pre * shared_slope).astype(jnp.bfloat16)
    shared_grad_up = (shared_grad_hidden * shared_act).astype(jnp.bfloat16)
    shared_input = jnp.dot(shared_grad_gate, shared_gate, preferred_element_type=jnp.float32)
    shared_input = shared_input + jnp.dot(
        shared_grad_up, shared_up, preferred_element_type=jnp.float32
    )
    value_back, input_back = (
        lax.all_to_all(value_part, "expert", split_axis=0, concat_axis=0, tiled=True),
        lax.all_to_all(input_part, "expert", split_axis=0, concat_axis=0, tiled=True),
    )
    early_value = shared_value + jnp.einsum(
        "st,sd->td",
        gate_dispatch,
        value_back.astype(jnp.float32),
        precision=lax.Precision.HIGHEST,
        preferred_element_type=jnp.float32,
    )
    early_input = shared_input + jnp.einsum(
        "st,sd->td",
        dispatch,
        input_back,
        precision=lax.Precision.HIGHEST,
        preferred_element_type=jnp.float32,
    )
    value_total, input_total = (
        lax.psum_scatter(early_value, "tensor", scatter_dimension=1, tiled=True),
        lax.psum_scatter(early_input, "tensor", scatter_dimension=1, tiled=True),
    )
    return (value_total.astype(jnp.bfloat16), input_total.astype(jnp.bfloat16))


def solution(mesh):
    in_specs = (
        P("expert", "tensor"),
        P("expert", "tensor"),
        P("expert", None),
        P("expert", None),
        P("tensor", None),
        P("tensor", None),
        P("tensor", None),
        P("expert", "tensor", None),
        P("expert", "tensor", None),
        P("expert", "tensor", None),
    )
    out_specs = (P("expert", "tensor"), P("expert", "tensor"))
    return jax.shard_map(
        on_device, mesh=mesh, in_specs=in_specs, out_specs=out_specs, check_vma=False
    )
```

profile of v0, /device:TPU:0, one launch (start us, length us, event | category | flops | bytes accessed | tf_op | source)
XLA Modules:
  0.0 222.2 jit_solution(5177407489219410796)
XLA Ops:
  7.2 0.9 copy.19
  8.1 0.1 eq.50
  8.3 0.1 eq.46
  8.4 0.7 broadcast_multiply_fusion
  9.1 1.7 reduce-window.6
  10.8 0.3 slice_reduce_fusion
  11.1 0.1 fusion.35
  11.2 0.1 reduce_sum.21
  11.4 0.1 copy.23
  11.5 0.1 copy.24
  11.5 0.2 fusion.16
  11.7 2.3 %convolution_convert_fusion = bf16[384,1024]{1,0:T(8,128)(2,1)} fusion(pred[384,128]{1,0:T(8,128)(4,1)S(1)} %fusion.16, bf16[128,1024]{1,0:T(8,128)(2,1)} %param.10), kind=kOutput, calls=%fused_computation.18 | convolution fusion | flops 101056512 | bytes 1097728 | tf_op jit(solution)/shard_map/dot_general | solution.py:48
  14.0 7.4 %all-to-all-start = ((bf16[16,24,1024]{2,1,0:T(8,128)(2,1)}), bf16[16,24,1024]{2,1,0:T(8,128)(2,1)}, u32[]{:S(2)}, u32[]{:S(2)}) async-start(bf16[16,24,1024]{2,1,0:T(8,128)(2,1)} %bitcast.74), calls=%async_computation | async-start | bytes 1572864 | tf_op jit(solution)/shard_map/all_to_all | solution.py:53
  21.4 0.0 all-gather.3.cloned.1.call-start
  21.5 0.1 copy.25
  21.6 0.1 broadcast_in_dim.27
  21.7 0.2 select_reduce_fusion
  21.9 18.2 %all-to-all-done = bf16[16,24,1024]{2,1,0:T(8,128)(2,1)} async-done(((bf16[16,24,1024]{2,1,0:T(8,128)(2,1)}), bf16[16,24,1024]{2,1,0:T(8,128)(2,1)}, u32[]{:S(2)}, u32[]{:S(2)}) %all-to-all-start) | async-done | bytes 786464 | tf_op jit(solution)/shard_map/all_to_all | solution.py:53
  40.2 0.0 all-gather.5.cloned.1.call-start
  40.2 0.4 multiply_convert_fusion
  40.6 25.4 %all_to_all.48 = bf16[16,24,1024]{2,1,0:T(8,128)(2,1)} all-to-all(bf16[16,24,1024]{2,1,0:T(8,128)(2,1)S(1)} %bitcast.76), channel_id=1, replica_groups=mesh['expert'=16,'tensor'=2] {'expert'}, dimensions={0} | all-to-all | bytes 1572864 | tf_op jit(solution)/shard_map/all_to_all | solution.py:54
  66.0 2.2 %all-gather.3.cloned.1.call-done = bf16[384,2048]{1,0:T(8,128)(2,1)} async-done(((bf16[384,1024]{1,0:T(8,128)(2,1)}), bf16[384,2048]{1,0:T(8,128)(2,1)}) %all-gather.3.cloned.1.call-update) | async-done | bytes 1572880 | tf_op jit(solution)/shard_map/all_gather | solution.py:57
  68.3 5.1 %fusion.7 = f32[384,704]{0,1:T(8,128)} fusion(bf16[384,2048]{1,0:T(8,128)(2,1)} %all-gather.3.cloned.1.call-done, bf16[1,704,2048]{2,1,0:T(8,128)(2,1)} %param.18), kind=kOutput, calls=%fused_computation.8 | convolution fusion | flops 1107296256 | bytes 5537792 | tf_op jit(solution)/shard_map/erd,efd->erf/dot_general | solution.py:74
  73.4 2.7 %fusion.9 = f32[384,704]{0,1:T(8,128)} fusion(bf16[384,2048]{1,0:T(8,128)(2,1)S(1)} %copy-done.15, bf16[1,704,2048]{2,1,0:T(8,128)(2,1)S(1)} %copy-done.13), kind=kOutput, calls=%fused_computation.10 | convolution fusion | flops 1107296256 | bytes 5537792 | tf_op jit(solution)/shard_map/erd,efd->erf/dot_general | solution.py:73
  76.0 21.0 %all-gather.5.cloned.1.call-done = bf16[384,2048]{1,0:T(8,128)(2,1)} async-done(((bf16[384,1024]{1,0:T(8,128)(2,1)}), bf16[384,2048]{1,0:T(8,128)(2,1)}) %all-gather.5.cloned.1.call-update) | async-done | bytes 1572880 | tf_op jit(solution)/shard_map/all_gather | solution.py:58
  97.0 4.1 %fusion.21 = (bf16[1,384,704]{1,2,0:T(8,128)(2,1)S(1)}, bf16[1,384,704]{1,2,0:T(8,128)(2,1)S(1)}) fusion(f32[384,704]{0,1:T(8,128)} %fusion.9, f32[384,704]{0,1:T(8,128)} %fusion.7, bf16[384,2048]{1,0:T(8,128)(2,1)} %all-gather.5.cloned.1.call-done, bf16[1,704,2048]{2,1,0:T(8,128)(2,1)S(1)} %copy-done), kind=kOutput, calls=%fused_computation.32 | convolution fusion | flops 1110810624 | bytes 7700480 | tf_op jit(solution)/shard_map/erd,efd->erf/dot_general | solution.py:77
  101.2 3.7 %fusion.14 = bf16[384,2048]{1,0:T(8,128)(2,1)} fusion(bf16[1,704,2048]{2,1,0:T(8,128)(2,1)S(1)} %copy-done.12, bf16[1,704,2048]{2,1,0:T(8,128)(2,1)S(1)} %copy-done.14, bf16[1,384,704]{1,2,0:T(8,128)(2,1)S(1)} %get-tuple-element.3, bf16[1,384,704]{1,2,0:T(8,128)(2,1)S(1)} %get-tuple-element.2), kind=kOutput, calls=%fused_computation.13 | convolution fusion | flops 2229075968 | bytes 8421376 | tf_op jit(solution)/shard_map/erf,efd->erd/dot_general | solution.py:87
  104.9 5.8 %all-to-all-start.3 = ((bf16[16,24,2048]{2,1,0:T(8,128)(2,1)}), bf16[16,24,2048]{2,1,0:T(8,128)(2,1)}, u32[]{:S(2)}, u32[]{:S(2)}) async-start(bf16[16,24,2048]{2,1,0:T(8,128)(2,1)} %bitcast.78), calls=%async_computation.4 | async-start | bytes 3145728 | tf_op jit(solution)/shard_map/all_to_all | solution.py:109
  110.7 9.2 %all_gather.12 = bf16[128,2048]{1,0:T(8,128)(2,1)S(1)} all-gather(bf16[128,1024]{1,0:T(8,128)(2,1)S(1)} %copy-done.7), channel_id=1, replica_groups=mesh['expert'=16,'tensor'=2] {'tensor'}, dimensions={1}, use_global_device_ids=true | all-gather | bytes 786432 | tf_op jit(solution)/shard_map/all_gather | solution.py:45
  120.0 0.8 copy-done.4
  120.8 2.9 %fusion.44 = f32[128,704]{0,1:T(8,128)S(1)} fusion(bf16[128,2048]{1,0:T(8,128)(2,1)S(1)} %all_gather.12, bf16[704,2048]{1,0:T(8,128)(2,1)} %param.14), kind=kOutput, calls=%fused_computation.62 | convolution fusion | flops 369098752 | bytes 3768320 | tf_op jit(solution)/shard_map/td,fd->tf/dot_general | solution.py:91
  123.7 2.7 %fusion.11 = bf16[384,2048]{1,0:T(8,128)(2,1)} fusion(bf16[1,704,2048]{2,1,0:T(8,128)(2,1)S(1)} %copy-done, f32[384,704]{0,1:T(8,128)S(1)} %copy-done.16, f32[384,704]{0,1:T(8,128)S(1)} %copy-done.17), kind=kOutput, calls=%fused_computation.12 | convolution fusion | flops 1109704704 | bytes 6619136 | tf_op jit(solution)/shard_map/erf,efd->erd/dot_general | solution.py:81
  126.4 16.3 %all-to-all-done.3 = bf16[16,24,2048]{2,1,0:T(8,128)(2,1)} async-done(((bf16[16,24,2048]{2,1,0:T(8,128)(2,1)}), bf16[16,24,2048]{2,1,0:T(8,128)(2,1)}, u32[]{:S(2)}, u32[]{:S(2)}) %all-to-all-start.3) | async-done | bytes 1572896 | tf_op jit(solution)/shard_map/all_to_all | solution.py:109
  142.6 9.2 %all-to-all-start.1 = ((bf16[16,24,2048]{2,1,0:T(8,128)(2,1)}), bf16[16,24,2048]{2,1,0:T(8,128)(2,1)}, u32[]{:S(2)}, u32[]{:S(2)}) async-start(bf16[16,24,2048]{2,1,0:T(8,128)(2,1)} %bitcast.77), calls=%async_computation.1 | async-start | bytes 3145728 | tf_op jit(solution)/shard_map/all_to_all | solution.py:108
  151.9 3.0 %fusion.45 = f32[128,704]{0,1:T(8,128)S(1)} fusion(bf16[128,2048]{1,0:T(8,128)(2,1)} %copy-done.4, bf16[704,2048]{1,0:T(8,128)(2,1)} %param.15), kind=kOutput, calls=%fused_computation.63 | convolution fusion | flops 369098752 | bytes 3768320 | tf_op jit(solution)/shard_map/td,fd->tf/dot_general | solution.py:94
  154.9 9.4 %all_gather.14 = bf16[128,2048]{1,0:T(8,128)(2,1)S(1)} all-gather(bf16[128,1024]{1,0:T(8,128)(2,1)S(1)} %copy-done.8), channel_id=1, replica_groups=mesh['expert'=16,'tensor'=2] {'tensor'}, dimensions={1}, use_global_device_ids=true | all-gather | bytes 786432 | tf_op jit(solution)/shard_map/all_gather | solution.py:46
  164.3 0.9 fusion.46
  165.3 0.9 copy-done.2
  166.2 0.7 fusion.27
  166.9 2.0 fusion.47
  168.9 1.6 fusion.15
  170.6 13.1 %all-to-all-done.1 = bf16[16,24,2048]{2,1,0:T(8,128)(2,1)} async-done(((bf16[16,24,2048]{2,1,0:T(8,128)(2,1)}), bf16[16,24,2048]{2,1,0:T(8,128)(2,1)}, u32[]{:S(2)}, u32[]{:S(2)}) %all-to-all-start.1) | async-done | bytes 1572896 | tf_op jit(solution)/shard_map/all_to_all | solution.py:108
  183.7 2.6 %fusion.23 = f32[128,2048]{1,0:T(8,128)S(1)} fusion(bf16[384,2048]{1,0:T(8,128)(2,1)} %bitcast.7, f32[384]{0:T(512)S(1)} %copy-done.10, pred[384,128]{1,0:T(8,128)(4,1)S(1)} %fusion.16), kind=kOutput, calls=%fused_computation.38 | convolution fusion | flops 1208107008 | bytes 2672128 | tf_op jit(solution)/shard_map/st,sd->td/dot_general | solution.py:111
  186.3 3.4 %convolution_add_fusion.1 = f32[128,2048]{1,0:T(8,128)} fusion(f32[128,2048]{1,0:T(8,128)S(1)} %fusion.23, bf16[704,2048]{1,0:T(8,128)(2,1)} %param.16, f32[128,704]{0,1:T(8,128)S(1)} %copy-done.6, f32[128,704]{0,1:T(8,128)S(1)} %fusion.44), kind=kOutput, calls=%fused_computation.15 | convolution fusion | flops 369901568 | bytes 5701632 | tf_op jit(solution)/shard_map/dot_general | solution.py:97
  189.7 1.5 reduce-scatter.5.cloned.1.call-done
  191.2 1.8 convert_element_type.76
  193.0 20.9 %reduce-scatter.3.cloned.1.call-done = f32[128,1024]{1,0:T(8,128)} async-done(((f32[128,2048]{1,0:T(8,128)}), f32[128,1024]{1,0:T(8,128)}) %reduce-scatter.3.cloned.1.call-update) | async-done | bytes 524304 | tf_op jit(solution)/shard_map/reduce_scatter | solution.py:126
  213.9 1.8 convert_element_type.67
  (44 shorter events, 0.3 us)
Async XLA Ops:
  7.2 89.9 %copy-start = (bf16[1,704,2048]{2,1,0:T(8,128)(2,1)S(1)}, bf16[1,704,2048]{2,1,0:T(8,128)(2,1)}, u32[]{:S(2)}) copy-start(bf16[1,704,2048]{2,1,0:T(8,128)(2,1)} %param.19) | copy-start | bytes 8650756
  11.2 10.3 %copy-start.11 = (f32[128,6]{0,1:T(8,128)S(1)}, f32[128,6]{0,1:T(8,128)}, u32[]{:S(2)}) copy-start(f32[128,6]{0,1:T(8,128)} %param.13) | copy-start | bytes 9220
  11.7 28.5 %copy-start.8 = (bf16[128,1024]{1,0:T(8,128)(2,1)S(1)}, bf16[128,1024]{1,0:T(8,128)(2,1)}, u32[]{:S(2)}) copy-start(bf16[128,1024]{1,0:T(8,128)(2,1)} %param.11) | copy-start | bytes 786436
  14.0 26.2 %all-to-all-start = ((bf16[16,24,1024]{2,1,0:T(8,128)(2,1)}), bf16[16,24,1024]{2,1,0:T(8,128)(2,1)}, u32[]{:S(2)}, u32[]{:S(2)}) async-start(bf16[16,24,1024]{2,1,0:T(8,128)(2,1)} %bitcast.74), calls=%async_computation | async-start | bytes 1572864 | tf_op jit(solution)/shard_map/all_to_all | solution.py:53
  21.4 46.9 %all-gather.3.cloned.1.call-start = ((), (), s32[]{:S(2)}) async-start(), calls=%async_computation.6 | async-start | bytes 2359296 | tf_op jit(solution)/shard_map/all_gather | solution.py:57
  21.9 44.1 %copy-start.9 = (f32[384]{0:T(512)}, f32[384]{0:T(512)S(1)}, u32[]{:S(2)}) copy-start(f32[384]{0:T(512)S(1)} %select_reduce_fusion) | copy-start | bytes 4612
  40.2 56.9 %all-gather.5.cloned.1.call-start = ((), (), s32[]{:S(2)}) async-start(), calls=%async_computation.8 | async-start | bytes 2359296 | tf_op jit(solution)/shard_map/all_gather | solution.py:58
  68.3 5.1 %copy-start.13 = (bf16[1,704,2048]{2,1,0:T(8,128)(2,1)S(1)}, bf16[1,704,2048]{2,1,0:T(8,128)(2,1)}, u32[]{:S(2)}) copy-start(bf16[1,704,2048]{2,1,0:T(8,128)(2,1)} %param.17) | copy-start | bytes 8650756
  68.3 5.1 %copy-start.15 = (bf16[384,2048]{1,0:T(8,128)(2,1)S(1)}, bf16[384,2048]{1,0:T(8,128)(2,1)}, u32[]{:S(2)}) copy-start(bf16[384,2048]{1,0:T(8,128)(2,1)} %all-gather.3.cloned.1.call-done) | copy-start | bytes 4718596
  97.0 4.1 %copy-start.12 = (bf16[1,704,2048]{2,1,0:T(8,128)(2,1)S(1)}, bf16[1,704,2048]{2,1,0:T(8,128)(2,1)}, u32[]{:S(2)}) copy-start(bf16[1,704,2048]{2,1,0:T(8,128)(2,1)} %param.18) | copy-start | bytes 8650756
  97.0 4.2 %copy-start.14 = (bf16[1,704,2048]{2,1,0:T(8,128)(2,1)S(1)}, bf16[1,704,2048]{2,1,0:T(8,128)(2,1)}, u32[]{:S(2)}) copy-start(bf16[1,704,2048]{2,1,0:T(8,128)(2,1)} %param.17) | copy-start | bytes 8650756
  104.9 5.8 %copy-start.7 = (bf16[128,1024]{1,0:T(8,128)(2,1)S(1)}, bf16[128,1024]{1,0:T(8,128)(2,1)}, u32[]{:S(2)}) copy-start(bf16[128,1024]{1,0:T(8,128)(2,1)} %param.10) | copy-start | bytes 786436
  104.9 37.7 %all-to-all-start.3 = ((bf16[16,24,2048]{2,1,0:T(8,128)(2,1)}), bf16[16,24,2048]{2,1,0:T(8,128)(2,1)}, u32[]{:S(2)}, u32[]{:S(2)}) async-start(bf16[16,24,2048]{2,1,0:T(8,128)(2,1)} %bitcast.78), calls=%async_computation.4 | async-start | bytes 3145728 | tf_op jit(solution)/shard_map/all_to_all | solution.py:109
  120.0 0.8 copy-start.4
  120.8 2.9 %copy-start.16 = (f32[384,704]{0,1:T(8,128)S(1)}, f32[384,704]{0,1:T(8,128)}, u32[]{:S(2)}) copy-start(f32[384,704]{0,1:T(8,128)} %fusion.7) | copy-start | bytes 3244036
  120.8 2.9 %copy-start.17 = (f32[384,704]{0,1:T(8,128)S(1)}, f32[384,704]{0,1:T(8,128)}, u32[]{:S(2)}) copy-start(f32[384,704]{0,1:T(8,128)} %fusion.9) | copy-start | bytes 3244036
  142.6 41.1 %all-to-all-start.1 = ((bf16[16,24,2048]{2,1,0:T(8,128)(2,1)}), bf16[16,24,2048]{2,1,0:T(8,128)(2,1)}, u32[]{:S(2)}, u32[]{:S(2)}) async-start(bf16[16,24,2048]{2,1,0:T(8,128)(2,1)} %bitcast.77), calls=%async_computation.1 | async-start | bytes 3145728 | tf_op jit(solution)/shard_map/all_to_all | solution.py:108
  151.8 39.4 %reduce-scatter.5.cloned.1.call-start = ((), (), s32[]{:S(2)}) async-start(), calls=%async_computation.9 | async-start | bytes 1572864 | tf_op jit(solution)/shard_map/reduce_scatter | solution.py:127
  151.8 12.5 %copy-start.3 = (bf16[704,2048]{1,0:T(8,128)(2,1)S(1)}, bf16[704,2048]{1,0:T(8,128)(2,1)}, u32[]{:S(2)}) copy-start(bf16[704,2048]{1,0:T(8,128)(2,1)} %param.16) | copy-start | bytes 8650756
  154.9 10.4 %copy-start.5 = (f32[128,704]{0,1:T(8,128)}, f32[128,704]{0,1:T(8,128)S(1)}, u32[]{:S(2)}) copy-start(f32[128,704]{0,1:T(8,128)S(1)} %fusion.45) | copy-start | bytes 1081348
  164.3 1.8 copy-start.2
  166.2 2.8 %copy-start.1 = (bf16[704,2048]{1,0:T(8,128)(2,1)S(1)}, bf16[704,2048]{1,0:T(8,128)(2,1)}, u32[]{:S(2)}) copy-start(bf16[704,2048]{1,0:T(8,128)(2,1)} %param.15) | copy-start | bytes 8650756
  168.9 14.8 %copy-start.10 = (f32[384]{0:T(512)S(1)}, f32[384]{0:T(512)}, u32[]{:S(2)}) copy-start(f32[384]{0:T(512)} %copy-done.9) | copy-start | bytes 4612
  170.6 43.3 %reduce-scatter.3.cloned.1.call-start = ((), (), s32[]{:S(2)}) async-start(), calls=%async_computation.7 | async-start | bytes 1572864 | tf_op jit(solution)/shard_map/reduce_scatter | solution.py:126
  183.7 2.6 %copy-start.6 = (f32[128,704]{0,1:T(8,128)S(1)}, f32[128,704]{0,1:T(8,128)}, u32[]{:S(2)}) copy-start(f32[128,704]{0,1:T(8,128)} %copy-done.5) | copy-start | bytes 1081348
Sparse Core Ops, SparseCore 0:
  40.3 27.9 all-gather.2
  69.8 27.1 all-gather.4
  170.7 20.4 reduce-scatter.4
  193.3 20.5 reduce-scatter.2
where the time goes:
time: 223 us; the launch traced here: 222 us
  waiting for transfers between devices  93.2 us (42%)
  blocking collectives  44.1 us (20%)
  matrix products  38.1 us (17%)
  starting transfers between devices  22.5 us (10%)
  between operations  14 us (6%)
  other arithmetic  6.47 us (3%)
  local copies, waits for them, and re-layouts  3.77 us (2%)
    all_to_all x1, blocking collectives, on_device(): lax.all_to_all(g_slots, 'expert', split_axis=0, concat_axis=0, tiled=True)  25.4 us
    all_gather x1, waiting for transfers between devices, on_device(): lax.all_gather(g_part, 'tensor', axis=1, tiled=True)  21 us
    reduce_scatter x1, waiting for transfers between devices, on_device(): lax.psum_scatter(early_value, 'tensor', scatter_dimension=1, tiled=True)  20.9 us
    all_to_all x1, waiting for transfers between devices, on_device(): lax.all_to_all(x_slots, 'expert', split_axis=0, concat_axis=0, tiled=True)  18.2 us
    all_to_all x1, waiting for transfers between devices, on_device(): lax.all_to_all(input_part, 'expert', split_axis=0, concat_axis=0, tiled=T...  16.3 us
    all_to_all x1, waiting for transfers between devices, on_device(): lax.all_to_all(value_part, 'expert', split_axis=0, concat_axis=0, tiled=T...  13.1 us
    all_gather x1, blocking collectives, on_device(): lax.all_gather(cotangent, 'tensor', axis=1, tiled=True)  9.42 us
    all_gather x1, blocking collectives, on_device(): lax.all_gather(tokens, 'tensor', axis=1, tiled=True)  9.24 us
  transfers between devices with their start and end apart: 7, of which 7 were waited for; matrix products, arithmetic and copies ran while one was open for 14% of the time, Pallas kernels for 0%

commit v1 on v0

--- a/solution.py
+++ b/solution.py
@@ -55,7 +55,9 @@
     )
     x_recv, g_recv = (
         lax.all_gather(x_part, "tensor", axis=1, tiled=True),
-        lax.all_gather(g_part, "tensor", axis=1, tiled=True),
+        jnp.concatenate(
+            lax.all_to_all(jnp.stack([g_part] * lax.axis_size("tensor")), "tensor", 0, 0), axis=1
+        ),
     )
 
     def owner_layout(values):

time: 223 us -> 226 us (1.013)
  waiting for transfers between devices: 93.2 us -> 86.9 us
  starting transfers between devices: 22.5 us -> 27.9 us
  local copies, waits for them, and re-layouts: 3.77 us -> 7.12 us
  matrix products: 38.1 us -> 34.9 us
    all_gather x1 -> x0, waiting for transfers between devices: 21 us -> none  [on_device(): lax.all_gather(g_part, 'tensor', axis=1, tiled=True)]
    all_to_all x0 -> x1, waiting for transfers between devices: none -> 18 us  [on_device(): lax.all_to_all(g_slots, 'expert', split_axis=0, concat_axis=0, tiled=True)]
    all_to_all x0 -> x1, starting transfers between devices: none -> 5.42 us  [on_device(): lax.all_to_all(g_slots, 'expert', split_axis=0, concat_axis=0, tiled=True)]
    reshape x0 -> x1, local copies, waits for them, and re-layouts: none -> 2.59 us  [on_device(): jnp.concatenate(lax.all_to_all(jnp.stack([g_part] * lax.axis_size('tensor...]
  transfers between devices with their start and end apart: 7 -> 7, of which waited for: 7 -> 6; matrix products, arithmetic and copies ran while one was open for 14% -> 12% of each run, Pallas kernels for 0% -> 0%
where the time goes in v1:
time: 226 us; the launch traced here: 225 us
  waiting for transfers between devices  86.9 us (38%)
  blocking collectives  46 us (20%)
  matrix products  34.9 us (15%)
  starting transfers between devices  27.9 us (12%)
  between operations  14.1 us (6%)
  other arithmetic  7.98 us (4%)
  local copies, waits for them, and re-layouts  7.12 us (3%)
    all_to_all x1, blocking collectives, on_device(): lax.all_to_all(jnp.stack([g_part] * lax.axis_size('tensor')), 'tensor', 0...  27.3 us
    reduce_scatter x1, waiting for transfers between devices, on_device(): lax.psum_scatter(early_value, 'tensor', scatter_dimension=1, tiled=True)  20.9 us
    all_to_all x1, waiting for transfers between devices, on_device(): lax.all_to_all(g_slots, 'expert', split_axis=0, concat_axis=0, tiled=True)  18 us
    all_to_all x1, waiting for transfers between devices, on_device(): lax.all_to_all(x_slots, 'expert', split_axis=0, concat_axis=0, tiled=True)  16.4 us
    all_to_all x1, waiting for transfers between devices, on_device(): lax.all_to_all(input_part, 'expert', split_axis=0, concat_axis=0, tiled=T...  16.3 us
    all_to_all x1, waiting for transfers between devices, on_device(): lax.all_to_all(value_part, 'expert', split_axis=0, concat_axis=0, tiled=T...  13.1 us
    all_gather x1, blocking collectives, on_device(): lax.all_gather(cotangent, 'tensor', axis=1, tiled=True)  9.41 us
    all_gather x1, blocking collectives, on_device(): lax.all_gather(tokens, 'tensor', axis=1, tiled=True)  9.24 us
  transfers between devices with their start and end apart: 7, of which 6 were waited for; matrix products, arithmetic and copies ran while one was open for 12% of the time, Pallas kernels for 0%

profile of v1, /device:TPU:0, one launch (start us, length us, event | category | flops | bytes accessed | tf_op | source)
XLA Modules:
  0.0 224.8 jit_solution(6612554958952874614)
XLA Ops:
  7.2 0.9 copy.27
  8.1 0.1 eq.50
  8.3 0.1 eq.46
  8.4 0.7 broadcast_multiply_fusion
  9.1 1.7 reduce-window.6
  10.8 0.3 slice_reduce_fusion
  11.2 0.1 reduce_sum.21
  11.4 0.1 copy.31
  11.5 0.2 fusion.16
  11.7 2.2 convolution_convert_fusion
  13.9 7.4 %all-to-all-start = ((bf16[16,24,1024]{2,1,0:T(8,128)(2,1)}), bf16[16,24,1024]{2,1,0:T(8,128)(2,1)}, u32[]{:S(2)}, u32[]{:S(2)}) async-start(bf16[16,24,1024]{2,1,0:T(8,128)(2,1)} %bitcast.78), calls=%async_computation | async-start | bytes 1572864 | tf_op jit(solution)/shard_map/all_to_all | solution.py:53
  21.5 0.1 broadcast_in_dim.27
  21.6 0.2 select_reduce_fusion
  21.9 0.6 copy-done.10
  22.4 1.2 multiply_convert_fusion
  23.7 16.4 %all-to-all-done = bf16[16,24,1024]{2,1,0:T(8,128)(2,1)} async-done(((bf16[16,24,1024]{2,1,0:T(8,128)(2,1)}), bf16[16,24,1024]{2,1,0:T(8,128)(2,1)}, u32[]{:S(2)}, u32[]{:S(2)}) %all-to-all-start) | async-done | bytes 786464 | tf_op jit(solution)/shard_map/all_to_all | solution.py:53
  40.1 5.4 %all-to-all-start.2 = ((bf16[16,24,1024]{2,1,0:T(8,128)(2,1)}), bf16[16,24,1024]{2,1,0:T(8,128)(2,1)}, u32[]{:S(2)}, u32[]{:S(2)}) async-start(bf16[16,24,1024]{2,1,0:T(8,128)(2,1)} %bitcast.77), calls=%async_computation.3 | async-start | bytes 1572864 | tf_op jit(solution)/shard_map/all_to_all | solution.py:54
  45.6 0.7 all-gather.2.cloned.1.call-update
  46.3 18.0 %all-to-all-done.2 = bf16[16,24,1024]{2,1,0:T(8,128)(2,1)} async-done(((bf16[16,24,1024]{2,1,0:T(8,128)(2,1)}), bf16[16,24,1024]{2,1,0:T(8,128)(2,1)}, u32[]{:S(2)}, u32[]{:S(2)}) %all-to-all-start.2) | async-done | bytes 786464 | tf_op jit(solution)/shard_map/all_to_all | solution.py:54
  64.3 1.5 pad_maximum_fusion
  65.8 27.3 %all_to_all.50 = bf16[2,384,1024]{2,1,0:T(8,128)(2,1)} all-to-all(bf16[2,384,1024]{2,1,0:T(8,128)(2,1)S(1)} %pad_maximum_fusion), channel_id=1, replica_groups=mesh['expert'=16,'tensor'=2] {'tensor'}, dimensions={0} | all-to-all | bytes 3145728 | tf_op jit(solution)/shard_map/all_to_all | solution.py:59
  93.1 2.6 %copy.34 = bf16[384,2,1024]{0,2,1:T(8,128)(2,1)} copy(bf16[384,2,1024]{2,0,1:T(8,128)(2,1)} %bitcast.76) | data formatting | bytes 3145728 | tf_op jit(solution)/shard_map/reshape | solution.py:58
  95.7 4.1 %fusion.7 = f32[384,704]{0,1:T(8,128)S(1)} fusion(bf16[384,2048]{1,0:T(8,128)(2,1)} %all-gather.2.cloned.1.call-done, bf16[1,704,2048]{2,1,0:T(8,128)(2,1)} %param.18), kind=kOutput, calls=%fused_computation.8 | convolution fusion | flops 1107296256 | bytes 5537792 | tf_op jit(solution)/shard_map/erd,efd->erf/dot_general | solution.py:76
  99.9 1.7 fusion.9
  101.7 1.9 fusion.21
  103.6 0.1 copy-done.13
  103.8 3.8 %fusion.14 = bf16[384,2048]{1,0:T(8,128)(2,1)} fusion(bf16[1,704,2048]{2,1,0:T(8,128)(2,1)S(1)} %copy-done.13, bf16[1,704,2048]{2,1,0:T(8,128)(2,1)S(1)} %copy-done.14, bf16[1,384,704]{1,2,0:T(8,128)(2,1)S(1)} %get-tuple-element.3, bf16[1,384,704]{1,2,0:T(8,128)(2,1)S(1)} %get-tuple-element.2), kind=kOutput, calls=%fused_computation.13 | convolution fusion | flops 2229075968 | bytes 8421376 | tf_op jit(solution)/shard_map/erf,efd->erd/dot_general | solution.py:89
  107.5 5.8 %all-to-all-start.4 = ((bf16[16,24,2048]{2,1,0:T(8,128)(2,1)}), bf16[16,24,2048]{2,1,0:T(8,128)(2,1)}, u32[]{:S(2)}, u32[]{:S(2)}) async-start(bf16[16,24,2048]{2,1,0:T(8,128)(2,1)} %bitcast.80), calls=%async_computation.5 | async-start | bytes 3145728 | tf_op jit(solution)/shard_map/all_to_all | solution.py:111
  113.3 9.2 %all_gather.9 = bf16[128,2048]{1,0:T(8,128)(2,1)S(1)} all-gather(bf16[128,1024]{1,0:T(8,128)(2,1)S(1)} %copy-done.8), channel_id=1, replica_groups=mesh['expert'=16,'tensor'=2] {'tensor'}, dimensions={1}, use_global_device_ids=true | all-gather | bytes 786432 | tf_op jit(solution)/shard_map/all_gather | solution.py:45
  122.6 0.8 copy-done.4
  123.4 2.9 %fusion.44 = f32[128,704]{0,1:T(8,128)S(1)} fusion(bf16[128,2048]{1,0:T(8,128)(2,1)S(1)} %all_gather.9, bf16[704,2048]{1,0:T(8,128)(2,1)} %param.14), kind=kOutput, calls=%fused_computation.63 | convolution fusion | flops 369098752 | bytes 3768320 | tf_op jit(solution)/shard_map/td,fd->tf/dot_general | solution.py:93
  126.3 2.7 %fusion.11 = bf16[384,2048]{1,0:T(8,128)(2,1)} fusion(bf16[1,704,2048]{2,1,0:T(8,128)(2,1)S(1)} %copy-done, f32[384,704]{0,1:T(8,128)S(1)} %copy-done.17, f32[384,704]{0,1:T(8,128)S(1)} %copy-done.19), kind=kOutput, calls=%fused_computation.12 | convolution fusion | flops 1109704704 | bytes 6619136 | tf_op jit(solution)/shard_map/erf,efd->erd/dot_general | solution.py:83
  128.9 16.3 %all-to-all-done.4 = bf16[16,24,2048]{2,1,0:T(8,128)(2,1)} async-done(((bf16[16,24,2048]{2,1,0:T(8,128)(2,1)}), bf16[16,24,2048]{2,1,0:T(8,128)(2,1)}, u32[]{:S(2)}, u32[]{:S(2)}) %all-to-all-start.4) | async-done | bytes 1572896 | tf_op jit(solution)/shard_map/all_to_all | solution.py:111
  145.2 9.2 %all-to-all-start.1 = ((bf16[16,24,2048]{2,1,0:T(8,128)(2,1)}), bf16[16,24,2048]{2,1,0:T(8,128)(2,1)}, u32[]{:S(2)}, u32[]{:S(2)}) async-start(bf16[16,24,2048]{2,1,0:T(8,128)(2,1)} %bitcast.79), calls=%async_computation.1 | async-start | bytes 3145728 | tf_op jit(solution)/shard_map/all_to_all | solution.py:110
  154.4 3.0 %fusion.45 = f32[128,704]{0,1:T(8,128)S(1)} fusion(bf16[128,2048]{1,0:T(8,128)(2,1)} %copy-done.4, bf16[704,2048]{1,0:T(8,128)(2,1)} %param.15), kind=kOutput, calls=%fused_computation.64 | convolution fusion | flops 369098752 | bytes 3768320 | tf_op jit(solution)/shard_map/td,fd->tf/dot_general | solution.py:96
  157.5 9.4 %all_gather.11 = bf16[128,2048]{1,0:T(8,128)(2,1)S(1)} all-gather(bf16[128,1024]{1,0:T(8,128)(2,1)S(1)} %copy-done.9), channel_id=1, replica_groups=mesh['expert'=16,'tensor'=2] {'tensor'}, dimensions={1}, use_global_device_ids=true | all-gather | bytes 786432 | tf_op jit(solution)/shard_map/all_gather | solution.py:46
  166.9 0.9 fusion.46
  167.9 0.9 copy-done.2
  168.7 0.7 fusion.27
  169.4 2.1 fusion.47
  171.5 1.6 fusion.15
  173.2 13.1 %all-to-all-done.1 = bf16[16,24,2048]{2,1,0:T(8,128)(2,1)} async-done(((bf16[16,24,2048]{2,1,0:T(8,128)(2,1)}), bf16[16,24,2048]{2,1,0:T(8,128)(2,1)}, u32[]{:S(2)}, u32[]{:S(2)}) %all-to-all-start.1) | async-done | bytes 1572896 | tf_op jit(solution)/shard_map/all_to_all | solution.py:110
  186.3 2.6 %fusion.23 = f32[128,2048]{1,0:T(8,128)S(1)} fusion(bf16[384,2048]{1,0:T(8,128)(2,1)} %bitcast.7, f32[384]{0:T(512)S(1)} %copy-done.11, pred[384,128]{1,0:T(8,128)(4,1)S(1)} %fusion.16), kind=kOutput, calls=%fused_computation.39 | convolution fusion | flops 1208107008 | bytes 2672128 | tf_op jit(solution)/shard_map/st,sd->td/dot_general | solution.py:113
  188.9 3.5 %convolution_add_fusion.1 = f32[128,2048]{1,0:T(8,128)} fusion(f32[128,2048]{1,0:T(8,128)S(1)} %fusion.23, bf16[704,2048]{1,0:T(8,128)(2,1)} %param.16, f32[128,704]{0,1:T(8,128)S(1)} %copy-done.6, f32[128,704]{0,1:T(8,128)S(1)} %fusion.44), kind=kOutput, calls=%fused_computation.15 | convolution fusion | flops 369901568 | bytes 5701632 | tf_op jit(solution)/shard_map/dot_general | solution.py:99
  192.4 1.5 reduce-scatter.5.cloned.1.call-done
  193.8 1.8 convert_element_type.76
  195.6 20.9 %reduce-scatter.3.cloned.1.call-done = f32[128,1024]{1,0:T(8,128)} async-done(((f32[128,2048]{1,0:T(8,128)}), f32[128,1024]{1,0:T(8,128)}) %reduce-scatter.3.cloned.1.call-update) | async-done | bytes 524304 | tf_op jit(solution)/shard_map/reduce_scatter | solution.py:128
  216.5 1.8 convert_element_type.67
  (49 shorter events, 0.6 us)
Async XLA Ops:
  7.2 94.4 %copy-start = (bf16[1,704,2048]{2,1,0:T(8,128)(2,1)S(1)}, bf16[1,704,2048]{2,1,0:T(8,128)(2,1)}, u32[]{:S(2)}) copy-start(bf16[1,704,2048]{2,1,0:T(8,128)(2,1)} %param.19) | copy-start | bytes 8650756
  11.2 10.2 %copy-start.12 = (f32[128,6]{0,1:T(8,128)S(1)}, f32[128,6]{0,1:T(8,128)}, u32[]{:S(2)}) copy-start(f32[128,6]{0,1:T(8,128)} %param.13) | copy-start | bytes 9220
  11.5 11.0 %copy-start.9 = (bf16[128,1024]{1,0:T(8,128)(2,1)S(1)}, bf16[128,1024]{1,0:T(8,128)(2,1)}, u32[]{:S(2)}) copy-start(bf16[128,1024]{1,0:T(8,128)(2,1)} %param.11) | copy-start | bytes 786436
  13.9 26.2 %all-to-all-start = ((bf16[16,24,1024]{2,1,0:T(8,128)(2,1)}), bf16[16,24,1024]{2,1,0:T(8,128)(2,1)}, u32[]{:S(2)}, u32[]{:S(2)}) async-start(bf16[16,24,1024]{2,1,0:T(8,128)(2,1)} %bitcast.78), calls=%async_computation | async-start | bytes 1572864 | tf_op jit(solution)/shard_map/all_to_all | solution.py:53
  21.9 0.6 copy-start.10
  40.1 24.2 %all-to-all-start.2 = ((bf16[16,24,1024]{2,1,0:T(8,128)(2,1)}), bf16[16,24,1024]{2,1,0:T(8,128)(2,1)}, u32[]{:S(2)}, u32[]{:S(2)}) async-start(bf16[16,24,1024]{2,1,0:T(8,128)(2,1)} %bitcast.77), calls=%async_computation.3 | async-start | bytes 1572864 | tf_op jit(solution)/shard_map/all_to_all | solution.py:54
  45.5 50.2 %all-gather.2.cloned.1.call-start = ((), (), s32[]{:S(2)}) async-start(), calls=%async_computation.7 | async-start | bytes 2359296 | tf_op jit(solution)/shard_map/all_gather | solution.py:57
  95.7 4.1 %copy-start.14 = (bf16[1,704,2048]{2,1,0:T(8,128)(2,1)S(1)}, bf16[1,704,2048]{2,1,0:T(8,128)(2,1)}, u32[]{:S(2)}) copy-start(bf16[1,704,2048]{2,1,0:T(8,128)(2,1)} %param.17) | copy-start | bytes 8650756
  95.7 4.1 %copy-start.15 = (bf16[384,2048]{1,0:T(8,128)(2,1)S(1)}, bf16[384,2048]{1,0:T(8,128)(2,1)}, u32[]{:S(2)}) copy-start(bf16[384,2048]{1,0:T(8,128)(2,1)} %all-gather.2.cloned.1.call-done) | copy-start | bytes 4718596
  99.8 1.7 copy-start.16
  99.9 1.8 copy-start.7
  101.5 2.1 copy-start.18
  101.7 2.1 copy-start.13
  107.5 5.8 %copy-start.8 = (bf16[128,1024]{1,0:T(8,128)(2,1)S(1)}, bf16[128,1024]{1,0:T(8,128)(2,1)}, u32[]{:S(2)}) copy-start(bf16[128,1024]{1,0:T(8,128)(2,1)} %param.10) | copy-start | bytes 786436
  107.5 37.7 %all-to-all-start.4 = ((bf16[16,24,2048]{2,1,0:T(8,128)(2,1)}), bf16[16,24,2048]{2,1,0:T(8,128)(2,1)}, u32[]{:S(2)}, u32[]{:S(2)}) async-start(bf16[16,24,2048]{2,1,0:T(8,128)(2,1)} %bitcast.80), calls=%async_computation.5 | async-start | bytes 3145728 | tf_op jit(solution)/shard_map/all_to_all | solution.py:111
  122.6 0.8 copy-start.4
  123.4 2.9 %copy-start.17 = (f32[384,704]{0,1:T(8,128)S(1)}, f32[384,704]{0,1:T(8,128)}, u32[]{:S(2)}) copy-start(f32[384,704]{0,1:T(8,128)} %copy-done.16) | copy-start | bytes 3244036
  123.4 2.9 %copy-start.19 = (f32[384,704]{0,1:T(8,128)S(1)}, f32[384,704]{0,1:T(8,128)}, u32[]{:S(2)}) copy-start(f32[384,704]{0,1:T(8,128)} %copy-done.18) | copy-start | bytes 3244036
  145.2 41.1 %all-to-all-start.1 = ((bf16[16,24,2048]{2,1,0:T(8,128)(2,1)}), bf16[16,24,2048]{2,1,0:T(8,128)(2,1)}, u32[]{:S(2)}, u32[]{:S(2)}) async-start(bf16[16,24,2048]{2,1,0:T(8,128)(2,1)} %bitcast.79), calls=%async_computation.1 | async-start | bytes 3145728 | tf_op jit(solution)/shard_map/all_to_all | solution.py:110
  154.4 39.4 %reduce-scatter.5.cloned.1.call-start = ((), (), s32[]{:S(2)}) async-start(), calls=%async_computation.9 | async-start | bytes 1572864 | tf_op jit(solution)/shard_map/reduce_scatter | solution.py:129
  154.4 12.5 %copy-start.3 = (bf16[704,2048]{1,0:T(8,128)(2,1)S(1)}, bf16[704,2048]{1,0:T(8,128)(2,1)}, u32[]{:S(2)}) copy-start(bf16[704,2048]{1,0:T(8,128)(2,1)} %param.16) | copy-start | bytes 8650756
  157.5 10.4 %copy-start.5 = (f32[128,704]{0,1:T(8,128)}, f32[128,704]{0,1:T(8,128)S(1)}, u32[]{:S(2)}) copy-start(f32[128,704]{0,1:T(8,128)S(1)} %fusion.45) | copy-start | bytes 1081348
  166.9 1.8 copy-start.2
  168.7 2.8 %copy-start.1 = (bf16[704,2048]{1,0:T(8,128)(2,1)S(1)}, bf16[704,2048]{1,0:T(8,128)(2,1)}, u32[]{:S(2)}) copy-start(bf16[704,2048]{1,0:T(8,128)(2,1)} %param.15) | copy-start | bytes 8650756
  171.5 14.8 %copy-start.11 = (f32[384]{0:T(512)S(1)}, f32[384]{0:T(512)}, u32[]{:S(2)}) copy-start(f32[384]{0:T(512)} %copy-done.10) | copy-start | bytes 4612
  173.2 43.3 %reduce-scatter.3.cloned.1.call-start = ((), (), s32[]{:S(2)}) async-start(), calls=%async_computation.8 | async-start | bytes 1572864 | tf_op jit(solution)/shard_map/reduce_scatter | solution.py:128
  186.3 2.6 %copy-start.6 = (f32[128,704]{0,1:T(8,128)S(1)}, f32[128,704]{0,1:T(8,128)}, u32[]{:S(2)}) copy-start(f32[128,704]{0,1:T(8,128)} %copy-done.5) | copy-start | bytes 1081348
Sparse Core Ops, SparseCore 0:
  47.9 32.5 all-gather.1
  173.3 20.4 reduce-scatter.4
  196.1 20.3 reduce-scatter.2
